TPU v7x, 32 devices: a whole 2x2x4 slice. The times are simulated.
32 devices in a mesh: row: 8 (over y, x, core), col: 4 (over z).
Axes of the slice: x: 2, y: 2, z: 4, core: 2. Of those that a mesh axis runs over, the one named last changes fastest.
Arguments:
- mode_block: float32 [32768, 256], P(('row', 'col')), may hold values from -80 to 80
- k_blocks: float32 [256, 3, 128, 128], P(('row', 'col')), may hold values from -1 to 9
- block_cols: int32 [256, 3], P(('row', 'col')), may hold values from 0 to 255, as said below
- panel_node: int32 [4096], replicated, may hold values from 0 to 32767, as said below
- added_mass: bfloat16 [4096, 4096], P('row', 'col'), may hold values from -0.125 to 0.125
- low_edge: int32 [256], replicated, may hold values from 4 to 8
- high_edge: int32 [256], replicated, may hold values from 40 to 56
Outputs:
- filtered: float32 [32768, 256], P(('row', 'col'))
Inputs may be any that keep to these rules, and one draw needn't show every extreme that they name: `panel_node`: distinct shell rows. Cut the panels into 32 aligned blocks of 128; in each block at most 8 panels lie on the 1024 rows of one shell device (rows d * 1024 to (d + 1) * 1024 - 1), exactly 8 for some device, and the panels of a block on one device are consecutive. `block_cols`: row i holds i first, then two different block rows among i - 2 to i + 2 other than i.
All inputs are finite; a program needn't handle non-finite values.
Results may differ from a plain program's by a relative error of at most 0.0015.
Values may be sent and summed in bfloat16 or wider, within the bound.
A program may use at most 64 MiB of HBM per device.

v0:
```python
import jax
import jax.numpy as jnp
from jax import lax
from jax.sharding import PartitionSpec as P

DEGREE = 3
OUTER = 2


def with_halo(block, sides, width):
    for axis, dim in sides:
        count = lax.axis_size(axis)
        forward = [(i, i + 1) for i in range(count - 1)]
        backward = [(target, source) for source, target in forward]
        low = lax.ppermute(
            lax.slice_in_dim(block, block.shape[dim] - width, None, axis=dim), axis, forward
        )
        high = lax.ppermute(lax.slice_in_dim(block, 0, width, axis=dim), axis, backward)
        block = jnp.concatenate([low, block, high], axis=dim)
    return block


def body(mode_block, k_blocks, block_cols, panel_node, added_mass, low_edge, high_edge):
    n_row = lax.axis_size("row")
    n_col = lax.axis_size("col")
    devices = n_row * n_col
    my_row = lax.axis_index("row")
    my_col = lax.axis_index("col")
    linear = my_row * n_col + my_col
    rows_dev = mode_block.shape[0]
    mode_width = mode_block.shape[1]
    block_size = k_blocks.shape[2]
    blocks_dev = rows_dev // block_size
    panel_count = panel_node.shape[0]
    per_block = panel_count // devices
    slot_count = 2 * ((per_block + devices - 1) // devices)
    flat_total = devices * slot_count
    panel_rows = panel_node.reshape(devices, per_block)
    source = panel_rows // rows_dev
    within = jnp.arange(per_block)
    earlier = within[None, :] < within[:, None]
    same_source = source[:, :, None] == source[:, None, :]
    slot_rank = jnp.sum((same_source & earlier[None, :, :]).astype(jnp.int32), axis=2)
    block_ids = jnp.arange(devices)[:, None]
    target = block_ids % n_row * n_col + block_ids // n_row
    owned = source == linear
    local_row = panel_rows - linear * rows_dev
    send_flat = jnp.where(owned, target * slot_count + slot_rank, flat_total)
    send_index = jnp.full((flat_total,), rows_dev, dtype=jnp.int32)
    send_index = send_index.at[send_flat.reshape(-1)].set(local_row.reshape(-1), mode="drop")
    return_rows = jnp.where(owned, local_row, rows_dev)
    return_index = jnp.full((rows_dev,), flat_total, dtype=jnp.int32)
    return_index = return_index.at[return_rows.reshape(-1)].set(
        (block_ids * slot_count + slot_rank).reshape(-1), mode="drop"
    )
    in_block = my_col * n_row + my_row
    in_source = lax.dynamic_index_in_dim(source, in_block, 0, keepdims=False)
    in_slot = lax.dynamic_index_in_dim(slot_rank, in_block, 0, keepdims=False)
    in_flat = in_source * slot_count + in_slot
    out_source = lax.dynamic_index_in_dim(source, linear, 0, keepdims=False)
    out_slot = lax.dynamic_index_in_dim(slot_rank, linear, 0, keepdims=False)
    out_index = jnp.full((flat_total,), per_block, dtype=jnp.int32)
    out_index = out_index.at[out_source * slot_count + out_slot].set(within)
    row_source = lax.dynamic_slice_in_dim(source, my_row * n_col, n_col, 0)
    row_slot = lax.dynamic_slice_in_dim(slot_rank, my_row * n_col, n_col, 0)
    row_flat = (
        row_source * (n_col * slot_count) + jnp.arange(n_col)[:, None] * slot_count + row_slot
    )
    part_index = jnp.full((devices * n_col * slot_count,), n_col * per_block, dtype=jnp.int32)
    part_index = part_index.at[row_flat.reshape(-1)].set(jnp.arange(n_col * per_block))
    local_cols = block_cols - (linear * blocks_dev - 2)
    zero_bf = jnp.zeros((1, mode_width), jnp.bfloat16)
    zero_row = jnp.zeros((1, mode_width), jnp.float32)

    def stiffness(vectors):
        padded = with_halo(vectors, ((("row", "col"), 0),), 2 * block_size)
        pieces = padded.reshape(blocks_dev + 4, block_size, mode_width)
        chosen = pieces[local_cols]
        product = jnp.einsum("rkij,rkjn->rin", k_blocks, chosen, precision=lax.Precision.HIGHEST)
        return product.reshape(rows_dev, mode_width)

    def accumulate(arrived_piece):
        return jnp.dot(added_mass, arrived_piece, preferred_element_type=jnp.float32)

    def fluid_loads(vectors):
        rounded = jnp.concatenate([vectors.astype(jnp.bfloat16), zero_bf], axis=0)
        outgoing = rounded[send_index]
        arrived = lax.all_to_all(
            outgoing.reshape(devices, slot_count, mode_width),
            ("row", "col"),
            split_axis=0,
            concat_axis=0,
            tiled=True,
        )
        arrived = arrived.reshape(flat_total, mode_width)
        wetted = arrived[in_flat]
        partial_value = accumulate(lax.all_gather(wetted, "row", axis=0, tiled=True))
        pressure = lax.psum_scatter(partial_value, "col", scatter_dimension=0, tiled=True)
        padded_press = jnp.concatenate([pressure, zero_row], axis=0)
        sending = padded_press[out_index].reshape(devices, slot_count, mode_width)
        summed = lax.all_to_all(
            sending, ("row", "col"), split_axis=0, concat_axis=0, tiled=True
        ).reshape(flat_total, mode_width)
        padded_sum = jnp.concatenate([summed, zero_row], axis=0)
        return padded_sum[return_index]

    def operate(vectors):
        return stiffness(vectors) + fluid_loads(vectors)

    lower = low_edge.astype(jnp.float32) * 0.25
    upper = high_edge.astype(jnp.float32) * 0.25
    centre = 0.5 * (upper + lower)
    radius = 0.5 * (upper - lower)
    total_rows = rows_dev * devices
    current = mode_block
    for outer_no in range(OUTER):
        previous = current
        current = (operate(current) - centre * current) / radius
        for degree_no in range(DEGREE - 1):
            following = 2.0 * (operate(current) - centre * current) / radius - previous
            previous = current
            current = following
        squares = lax.psum(jnp.sum(current * current, axis=0), ("row", "col"))
        current = current / jnp.sqrt(squares / total_rows + 1e-06)
    return current


def solution(mesh):
    placed = (
        P(("row", "col"), None),
        P(("row", "col"), None, None, None),
        P(("row", "col"), None),
        P(),
        P("row", "col"),
        P(),
        P(),
    )
    return jax.shard_map(
        body, mesh=mesh, in_specs=placed, out_specs=P(("row", "col"), None), check_vma=False
    )
```

profile of v0, /device:TPU:0, one launch (start us, length us, event | category | flops | bytes accessed | tf_op | source)
XLA Modules:
  0.0 587.0 jit_solution(11731140511086322295)
XLA Ops:
  9.5 15.5 %scatter_custom_fusion = s32[256]{0:T(256)S(1)} fusion(s32[4096]{0:T(1024)S(1)} %get-tuple-element.35, s32[4096]{0:T(1024)S(1)} %get-tuple-element.20, s32[]{:T(128)} %constant.94.clone.1), kind=kCustom, calls=%fused_computation.139 | custom fusion | bytes 1028 | tf_op jit(solution)/shard_map/scatter | solution.py:50
  28.2 7.3 %all-to-all-start = ((bf16[32,8,256]{2,1,0:T(8,128)(2,1)}), bf16[32,8,256]{2,1,0:T(8,128)(2,1)S(1)}, u32[]{:S(2)}, u32[]{:S(2)}) async-start(bf16[32,8,256]{2,1,0:T(8,128)(2,1)} %bitcast.8), calls=%async_computation | async-start | bytes 262144 | tf_op jit(solution)/shard_map/all_to_all | solution.py:88
  37.4 3.7 collective-permute-start
  44.8 13.9 %all-gather = bf16[1024,256]{1,0:T(8,128)(2,1)S(1)} all-gather(bf16[128,256]{1,0:T(8,128)(2,1)S(1)} %gather_fusion.2), channel_id=2, replica_groups=mesh['row'=8,'col'=4] {'row'}, dimensions={0}, use_global_device_ids=true | all-gather | bytes 589824 | tf_op jit(solution)/shard_map/all_gather | solution.py:97
  60.3 15.5 %scatter_custom_fusion.2 = s32[1024]{0:T(1024)S(1)} fusion(s32[4096]{0:T(1024)S(1)} %get-tuple-element.19, s32[4096]{0:T(1024)S(1)} %add_bitcast_fusion, s32[]{:T(128)} %constant.101.clone.1), kind=kCustom, calls=%fused_computation.110 | custom fusion | bytes 4100 | tf_op jit(solution)/shard_map/scatter | solution.py:53
  75.8 4.1 reduce-scatter.7.cloned.1.call-done
  82.6 2.9 all-to-all-start.1
  85.5 2.6 pad_maximum_fusion
  88.1 3.8 gather_fusion
  91.9 5.1 fusion.59
  97.1 4.7 gather_fusion.4
  101.8 3.0 fusion.51
  106.0 14.0 %all_to_all.60 = bf16[32,8,256]{2,1,0:T(8,128)(2,1)S(1)} all-to-all(bf16[32,8,256]{2,1,0:T(8,128)(2,1)S(1)} %bitcast.215), channel_id=1, replica_groups=mesh['row'=8,'col'=4] {'row','col'}, dimensions={0} | all-to-all | bytes 262144 | tf_op jit(solution)/shard_map/all_to_all | solution.py:88
  120.9 9.3 %all-gather.1 = bf16[1024,256]{1,0:T(8,128)(2,1)S(1)} all-gather(bf16[128,256]{1,0:T(8,128)(2,1)S(1)} %gather_fusion.7), channel_id=3, replica_groups=mesh['row'=8,'col'=4] {'row'}, dimensions={0}, use_global_device_ids=true | all-gather | bytes 589824 | tf_op jit(solution)/shard_map/all_gather | solution.py:97
  131.5 1.9 fusion.57
  136.5 20.1 %reduce-scatter.9.cloned.1.call-done = f32[128,256]{0,1:T(8,128)} async-done(((f32[512,256]{0,1:T(8,128)}), f32[128,256]{0,1:T(8,128)}) %reduce-scatter.9.cloned.1.call-update) | async-done | bytes 131088 | tf_op jit(solution)/shard_map/reduce_scatter | solution.py:98
  159.2 4.6 all-to-all-start.3
  164.0 2.6 pad_maximum_fusion.1
  166.6 3.8 gather_fusion.5
  170.3 5.1 fusion.60
  175.5 4.7 gather_fusion.9
  180.2 3.4 fusion.49
  184.9 14.0 %all_to_all.61 = bf16[32,8,256]{2,1,0:T(8,128)(2,1)S(1)} all-to-all(bf16[32,8,256]{2,1,0:T(8,128)(2,1)S(1)} %bitcast.216), channel_id=1, replica_groups=mesh['row'=8,'col'=4] {'row','col'}, dimensions={0} | all-to-all | bytes 262144 | tf_op jit(solution)/shard_map/all_to_all | solution.py:88
  199.7 9.1 %all-gather.2 = bf16[1024,256]{1,0:T(8,128)(2,1)S(1)} all-gather(bf16[128,256]{1,0:T(8,128)(2,1)S(1)} %gather_fusion.12), channel_id=4, replica_groups=mesh['row'=8,'col'=4] {'row'}, dimensions={0}, use_global_device_ids=true | all-gather | bytes 589824 | tf_op jit(solution)/shard_map/all_gather | solution.py:97
  210.2 1.9 fusion.56
  215.1 20.1 %reduce-scatter.11.cloned.1.call-done = f32[128,256]{0,1:T(8,128)} async-done(((f32[512,256]{0,1:T(8,128)}), f32[128,256]{0,1:T(8,128)}) %reduce-scatter.11.cloned.1.call-update) | async-done | bytes 131088 | tf_op jit(solution)/shard_map/reduce_scatter | solution.py:98
  237.9 4.7 all-to-all-start.5
  243.0 2.6 pad_maximum_fusion.2
  245.6 3.8 gather_fusion.10
  249.4 5.1 fusion.61
  254.6 4.7 gather_fusion.14
  259.3 3.4 multiply_reduce_fusion.1
  262.7 40.4 %psum.14 = f32[256]{0:T(256)S(1)} all-reduce(f32[256]{0:T(256)S(1)} %get-tuple-element.13), channel_id=1, replica_groups=mesh['row'=8,'col'=4] {'row','col'}, use_global_device_ids=true, to_apply=%region_8.9 | all-reduce | flops 256 | bytes 2048 | tf_op jit(solution)/shard_map/psum | solution.py:123
  303.1 2.3 fusion.47
  306.6 12.7 %all_to_all.62 = bf16[32,8,256]{2,1,0:T(8,128)(2,1)S(1)} all-to-all(bf16[32,8,256]{2,1,0:T(8,128)(2,1)S(1)} %bitcast.217), channel_id=1, replica_groups=mesh['row'=8,'col'=4] {'row','col'}, dimensions={0} | all-to-all | bytes 262144 | tf_op jit(solution)/shard_map/all_to_all | solution.py:88
  320.1 9.1 %all-gather.3 = bf16[1024,256]{1,0:T(8,128)(2,1)S(1)} all-gather(bf16[128,256]{1,0:T(8,128)(2,1)S(1)} %gather_fusion.17), channel_id=5, replica_groups=mesh['row'=8,'col'=4] {'row'}, dimensions={0}, use_global_device_ids=true | all-gather | bytes 589824 | tf_op jit(solution)/shard_map/all_gather | solution.py:97
  330.6 1.9 fusion.55
  335.5 20.1 %reduce-scatter.13.cloned.1.call-done = f32[128,256]{0,1:T(8,128)} async-done(((f32[512,256]{0,1:T(8,128)}), f32[128,256]{0,1:T(8,128)}) %reduce-scatter.13.cloned.1.call-update) | async-done | bytes 131088 | tf_op jit(solution)/shard_map/reduce_scatter | solution.py:98
  358.3 4.6 all-to-all-start.7
  363.0 2.6 pad_maximum_fusion.3
  365.6 3.8 gather_fusion.15
  369.4 5.1 fusion.62
  374.5 4.7 gather_fusion.19
  379.3 3.1 fusion.45
  383.5 14.0 %all_to_all.63 = bf16[32,8,256]{2,1,0:T(8,128)(2,1)S(1)} all-to-all(bf16[32,8,256]{2,1,0:T(8,128)(2,1)S(1)} %bitcast.218), channel_id=1, replica_groups=mesh['row'=8,'col'=4] {'row','col'}, dimensions={0} | all-to-all | bytes 262144 | tf_op jit(solution)/shard_map/all_to_all | solution.py:88
  398.4 9.3 %all-gather.4 = bf16[1024,256]{1,0:T(8,128)(2,1)S(1)} all-gather(bf16[128,256]{1,0:T(8,128)(2,1)S(1)} %gather_fusion.22), channel_id=6, replica_groups=mesh['row'=8,'col'=4] {'row'}, dimensions={0}, use_global_device_ids=true | all-gather | bytes 589824 | tf_op jit(solution)/shard_map/all_gather | solution.py:97
  409.0 1.9 fusion.54
  414.0 20.1 %reduce-scatter.15.cloned.1.call-done = f32[128,256]{0,1:T(8,128)} async-done(((f32[512,256]{0,1:T(8,128)}), f32[128,256]{0,1:T(8,128)}) %reduce-scatter.15.cloned.1.call-update) | async-done | bytes 131088 | tf_op jit(solution)/shard_map/reduce_scatter | solution.py:98
  436.7 4.6 all-to-all-start.9
  441.4 2.6 pad_maximum_fusion.4
  444.0 3.8 gather_fusion.20
  447.8 5.1 fusion.63
  453.0 4.7 gather_fusion.24
  457.7 3.4 fusion.43
  462.3 14.0 %all_to_all.64 = bf16[32,8,256]{2,1,0:T(8,128)(2,1)S(1)} all-to-all(bf16[32,8,256]{2,1,0:T(8,128)(2,1)S(1)} %bitcast.214), channel_id=1, replica_groups=mesh['row'=8,'col'=4] {'row','col'}, dimensions={0} | all-to-all | bytes 262144 | tf_op jit(solution)/shard_map/all_to_all | solution.py:88
  477.1 9.1 %all-gather.5 = bf16[1024,256]{1,0:T(8,128)(2,1)S(1)} all-gather(bf16[128,256]{1,0:T(8,128)(2,1)S(1)} %gather_fusion.27), channel_id=7, replica_groups=mesh['row'=8,'col'=4] {'row'}, dimensions={0}, use_global_device_ids=true | all-gather | bytes 589824 | tf_op jit(solution)/shard_map/all_gather | solution.py:97
  491.7 21.1 %reduce-scatter.17.cloned.1.call-done = f32[128,256]{0,1:T(8,128)} async-done(((f32[512,256]{0,1:T(8,128)}), f32[128,256]{0,1:T(8,128)}) %reduce-scatter.17.cloned.1.call-update) | async-done | bytes 131088 | tf_op jit(solution)/shard_map/reduce_scatter | solution.py:98
  515.5 4.3 all-to-all-start.11
  519.8 2.5 pad_maximum_fusion.5
  522.3 3.8 gather_fusion.25
  526.1 5.1 fusion.64
  531.3 4.7 gather_fusion.29
  536.0 2.5 multiply_reduce_fusion
  538.4 40.5 %psum.15 = f32[256]{0:T(256)S(1)} all-reduce(f32[256]{0:T(256)S(1)} %get-tuple-element.5), channel_id=1, replica_groups=mesh['row'=8,'col'=4] {'row','col'}, use_global_device_ids=true, to_apply=%region_13.14 | all-reduce | flops 256 | bytes 2048 | tf_op jit(solution)/shard_map/psum | solution.py:123
  (127 shorter events, 64.0 us)
Async XLA Ops:
  6.5 85.4 %copy-start = (f32[8,3,128,128]{3,2,1,0:T(8,128)S(1)}, f32[8,3,128,128]{3,2,1,0:T(8,128)}, u32[]{:S(2)}) copy-start(f32[8,3,128,128]{3,2,1,0:T(8,128)} %param.8) | copy-start | bytes 4718596
  26.3 17.1 %copy-start.2 = (s32[8,3]{0,1:T(4,128)S(1)}, s32[8,3]{0,1:T(4,128)}, u32[]{:S(2)}) copy-start(s32[8,3]{0,1:T(4,128)} %param.9) | copy-start | bytes 292
  26.4 32.3 %copy-start.1 = (bf16[512,1024]{1,0:T(8,128)(2,1)S(1)}, bf16[512,1024]{1,0:T(8,128)(2,1)}, u32[]{:S(2)}) copy-start(bf16[512,1024]{1,0:T(8,128)(2,1)} %param.11) | copy-start | bytes 3145732
  28.2 15.7 %all-to-all-start = ((bf16[32,8,256]{2,1,0:T(8,128)(2,1)}), bf16[32,8,256]{2,1,0:T(8,128)(2,1)S(1)}, u32[]{:S(2)}, u32[]{:S(2)}) async-start(bf16[32,8,256]{2,1,0:T(8,128)(2,1)} %bitcast.8), calls=%async_computation | async-start | bytes 262144 | tf_op jit(solution)/shard_map/all_to_all | solution.py:88
  35.5 44.4 %reduce-scatter.7.cloned.1.call-start = ((), (), s32[]{:S(2)}) async-start(), calls=%async_computation.18 | async-start | bytes 655360 | tf_op jit(solution)/shard_map/reduce_scatter | solution.py:98
  37.4 48.1 %collective-permute-start = (f32[256,256]{1,0:T(8,128)}, f32[256,256]{1,0:T(8,128)S(1)}, u32[]{:S(2)}, u32[]{:S(2)}) collective-permute-start(f32[256,256]{1,0:T(8,128)} %get-tuple-element.31), channel_id=1, source_target_pairs={{0,1},{1,2},{2,3},{3,4},{4,5},{5,6},{6,7},{7,8},{8,9},{9,10},{10,1... | collective-permute-start | bytes 786440 | tf_op jit(solution)/shard_map/ppermute | solution.py:15
  41.1 44.4 %collective-permute-start.1 = (f32[256,256]{1,0:T(8,128)}, f32[256,256]{1,0:T(8,128)}, u32[]{:S(2)}, u32[]{:S(2)}) collective-permute-start(f32[256,256]{1,0:T(8,128)} %get-tuple-element.32), channel_id=1, source_target_pairs={{1,0},{2,1},{3,2},{4,3},{5,4},{6,5},{7,6},{8,7},{9,8},{10,9},{11,1... | collective-permute-start | bytes 786440 | tf_op jit(solution)/shard_map/ppermute | solution.py:18
  44.8 15.4 %copy-start.3 = (s32[256]{0:T(256)S(1)}, s32[256]{0:T(256)}, u32[]{:S(2)}) copy-start(s32[256]{0:T(256)} %param.13) | copy-start | bytes 3076
  44.8 15.4 %copy-start.4 = (s32[256]{0:T(256)S(1)}, s32[256]{0:T(256)}, u32[]{:S(2)}) copy-start(s32[256]{0:T(256)} %param.12) | copy-start | bytes 3076
  82.6 14.5 %all-to-all-start.1 = ((f32[32,8,256]{2,1,0:T(8,128)}), f32[32,8,256]{2,1,0:T(8,128)S(1)}, u32[]{:S(2)}, u32[]{:S(2)}) async-start(f32[32,8,256]{2,1,0:T(8,128)} %bitcast.15), calls=%async_computation.2 | async-start | bytes 524288 | tf_op jit(solution)/shard_map/all_to_all | solution.py:101
  85.5 71.1 %reduce-scatter.9.cloned.1.call-start = ((), (), s32[]{:S(2)}) async-start(), calls=%async_computation.19 | async-start | bytes 655360 | tf_op jit(solution)/shard_map/reduce_scatter | solution.py:98
  133.4 30.5 %collective-permute-start.2 = (f32[256,256]{1,0:T(8,128)}, f32[256,256]{1,0:T(8,128)S(1)}, u32[]{:S(2)}, u32[]{:S(2)}) collective-permute-start(f32[256,256]{1,0:T(8,128)} %get-tuple-element.29), channel_id=1, source_target_pairs={{0,1},{1,2},{2,3},{3,4},{4,5},{5,6},{6,7},{7,8},{8,9},{9,10},{10,1... | collective-permute-start | bytes 786440 | tf_op jit(solution)/shard_map/ppermute | solution.py:15
  135.2 28.8 %collective-permute-start.3 = (f32[256,256]{1,0:T(8,128)}, f32[256,256]{1,0:T(8,128)}, u32[]{:S(2)}, u32[]{:S(2)}) collective-permute-start(f32[256,256]{1,0:T(8,128)} %get-tuple-element.30), channel_id=1, source_target_pairs={{1,0},{2,1},{3,2},{4,3},{5,4},{6,5},{7,6},{8,7},{9,8},{10,9},{11,1... | collective-permute-start | bytes 786440 | tf_op jit(solution)/shard_map/ppermute | solution.py:18
  159.2 16.2 %all-to-all-start.3 = ((f32[32,8,256]{2,1,0:T(8,128)}), f32[32,8,256]{2,1,0:T(8,128)S(1)}, u32[]{:S(2)}, u32[]{:S(2)}) async-start(f32[32,8,256]{2,1,0:T(8,128)} %bitcast.27), calls=%async_computation.5 | async-start | bytes 524288 | tf_op jit(solution)/shard_map/all_to_all | solution.py:101
  163.9 71.3 %reduce-scatter.11.cloned.1.call-start = ((), (), s32[]{:S(2)}) async-start(), calls=%async_computation.20 | async-start | bytes 655360 | tf_op jit(solution)/shard_map/reduce_scatter | solution.py:98
  212.1 30.9 %collective-permute-start.4 = (f32[256,256]{1,0:T(8,128)}, f32[256,256]{1,0:T(8,128)S(1)}, u32[]{:S(2)}, u32[]{:S(2)}) collective-permute-start(f32[256,256]{1,0:T(8,128)} %get-tuple-element.27), channel_id=1, source_target_pairs={{0,1},{1,2},{2,3},{3,4},{4,5},{5,6},{6,7},{7,8},{8,9},{9,10},{10,1... | collective-permute-start | bytes 786440 | tf_op jit(solution)/shard_map/ppermute | solution.py:15
  213.8 29.2 %collective-permute-start.5 = (f32[256,256]{1,0:T(8,128)}, f32[256,256]{1,0:T(8,128)}, u32[]{:S(2)}, u32[]{:S(2)}) collective-permute-start(f32[256,256]{1,0:T(8,128)} %get-tuple-element.28), channel_id=1, source_target_pairs={{1,0},{2,1},{3,2},{4,3},{5,4},{6,5},{7,6},{8,7},{9,8},{10,9},{11,1... | collective-permute-start | bytes 786440 | tf_op jit(solution)/shard_map/ppermute | solution.py:18
  237.9 16.7 %all-to-all-start.5 = ((f32[32,8,256]{2,1,0:T(8,128)}), f32[32,8,256]{2,1,0:T(8,128)S(1)}, u32[]{:S(2)}, u32[]{:S(2)}) async-start(f32[32,8,256]{2,1,0:T(8,128)} %bitcast.38), calls=%async_computation.8 | async-start | bytes 524288 | tf_op jit(solution)/shard_map/all_to_all | solution.py:101
  242.6 113.1 %reduce-scatter.13.cloned.1.call-start = ((), (), s32[]{:S(2)}) async-start(), calls=%async_computation.21 | async-start | bytes 655360 | tf_op jit(solution)/shard_map/reduce_scatter | solution.py:98
  332.5 30.5 %collective-permute-start.6 = (f32[256,256]{1,0:T(8,128)}, f32[256,256]{1,0:T(8,128)S(1)}, u32[]{:S(2)}, u32[]{:S(2)}) collective-permute-start(f32[256,256]{1,0:T(8,128)} %get-tuple-element.25), channel_id=1, source_target_pairs={{0,1},{1,2},{2,3},{3,4},{4,5},{5,6},{6,7},{7,8},{8,9},{9,10},{10,1... | collective-permute-start | bytes 786440 | tf_op jit(solution)/shard_map/ppermute | solution.py:15
  334.2 28.8 %collective-permute-start.7 = (f32[256,256]{1,0:T(8,128)}, f32[256,256]{1,0:T(8,128)}, u32[]{:S(2)}, u32[]{:S(2)}) collective-permute-start(f32[256,256]{1,0:T(8,128)} %get-tuple-element.26), channel_id=1, source_target_pairs={{1,0},{2,1},{3,2},{4,3},{5,4},{6,5},{7,6},{8,7},{9,8},{10,9},{11,1... | collective-permute-start | bytes 786440 | tf_op jit(solution)/shard_map/ppermute | solution.py:18
  358.3 16.2 %all-to-all-start.7 = ((f32[32,8,256]{2,1,0:T(8,128)}), f32[32,8,256]{2,1,0:T(8,128)S(1)}, u32[]{:S(2)}, u32[]{:S(2)}) async-start(f32[32,8,256]{2,1,0:T(8,128)} %bitcast.49), calls=%async_computation.11 | async-start | bytes 524288 | tf_op jit(solution)/shard_map/all_to_all | solution.py:101
  362.9 71.1 %reduce-scatter.15.cloned.1.call-start = ((), (), s32[]{:S(2)}) async-start(), calls=%async_computation.22 | async-start | bytes 655360 | tf_op jit(solution)/shard_map/reduce_scatter | solution.py:98
  410.9 30.5 %collective-permute-start.8 = (f32[256,256]{1,0:T(8,128)}, f32[256,256]{1,0:T(8,128)S(1)}, u32[]{:S(2)}, u32[]{:S(2)}) collective-permute-start(f32[256,256]{1,0:T(8,128)} %get-tuple-element.23), channel_id=1, source_target_pairs={{0,1},{1,2},{2,3},{3,4},{4,5},{5,6},{6,7},{7,8},{8,9},{9,10},{10,1... | collective-permute-start | bytes 786440 | tf_op jit(solution)/shard_map/ppermute | solution.py:15
  412.7 28.7 %collective-permute-start.9 = (f32[256,256]{1,0:T(8,128)}, f32[256,256]{1,0:T(8,128)}, u32[]{:S(2)}, u32[]{:S(2)}) collective-permute-start(f32[256,256]{1,0:T(8,128)} %get-tuple-element.24), channel_id=1, source_target_pairs={{1,0},{2,1},{3,2},{4,3},{5,4},{6,5},{7,6},{8,7},{9,8},{10,9},{11,1... | collective-permute-start | bytes 786440 | tf_op jit(solution)/shard_map/ppermute | solution.py:18
  436.7 16.2 %all-to-all-start.9 = ((f32[32,8,256]{2,1,0:T(8,128)}), f32[32,8,256]{2,1,0:T(8,128)S(1)}, u32[]{:S(2)}, u32[]{:S(2)}) async-start(f32[32,8,256]{2,1,0:T(8,128)} %bitcast.60), calls=%async_computation.14 | async-start | bytes 524288 | tf_op jit(solution)/shard_map/all_to_all | solution.py:101
  441.4 71.5 %reduce-scatter.17.cloned.1.call-start = ((), (), s32[]{:S(2)}) async-start(), calls=%async_computation.23 | async-start | bytes 655360 | tf_op jit(solution)/shard_map/reduce_scatter | solution.py:98
  488.6 31.2 %collective-permute-start.10 = (f32[256,256]{1,0:T(8,128)S(1)}, f32[256,256]{1,0:T(8,128)S(1)}, u32[]{:S(2)}, u32[]{:S(2)}) collective-permute-start(f32[256,256]{1,0:T(8,128)S(1)} %get-tuple-element.21), channel_id=1, source_target_pairs={{0,1},{1,2},{2,3},{3,4},{4,5},{5,6},{6,7},{7,8},{8,9},{9,10},{10,1... | collective-permute-start | bytes 786440 | tf_op jit(solution)/shard_map/ppermute | solution.py:15
  490.4 29.4 %collective-permute-start.11 = (f32[256,256]{1,0:T(8,128)S(1)}, f32[256,256]{1,0:T(8,128)S(1)}, u32[]{:S(2)}, u32[]{:S(2)}) collective-permute-start(f32[256,256]{1,0:T(8,128)S(1)} %get-tuple-element.22), channel_id=1, source_target_pairs={{1,0},{2,1},{3,2},{4,3},{5,4},{6,5},{7,6},{8,7},{9,8},{10,9},{11,1... | collective-permute-start | bytes 786440 | tf_op jit(solution)/shard_map/ppermute | solution.py:18
  515.5 15.7 %all-to-all-start.11 = ((f32[32,8,256]{2,1,0:T(8,128)}), f32[32,8,256]{2,1,0:T(8,128)S(1)}, u32[]{:S(2)}, u32[]{:S(2)}) async-start(f32[32,8,256]{2,1,0:T(8,128)} %bitcast.71), calls=%async_computation.17 | async-start | bytes 524288 | tf_op jit(solution)/shard_map/all_to_all | solution.py:101
Sparse Core Ops, SparseCore 0:
  60.1 19.7 reduce-scatter.6
  131.6 24.8 reduce-scatter.8
  210.3 24.8 reduce-scatter.10
  330.7 24.8 reduce-scatter.12
  409.1 24.8 reduce-scatter.14
  487.7 25.0 reduce-scatter.16
where the time goes:
time: 597 us; the launch traced here: 587 us
  blocking collectives  209 us (35%)
  local copies, waits for them, and re-layouts  123 us (21%)
  waiting for transfers between devices  106 us (18%)
  starting transfers between devices  53.9 us (9%)
  other arithmetic  42.1 us (7%)
  matrix products  38.6 us (6%)
  between operations  14.3 us (2%)
    reduce_scatter x6, waiting for transfers between devices, fluid_loads(): lax.psum_scatter(partial_value, 'col', scatter_dimension=0, tiled=True)  105 us
    psum x2, blocking collectives, body(): squares = lax.psum(jnp.sum(current * current, axis=0), ('row', 'col'))  80.9 us
    all_to_all x5, blocking collectives, fluid_loads(): lax.all_to_all(outgoing.reshape(devices, slot_count, mode_width), ('row',...  68.7 us
    all_gather x6, blocking collectives, fluid_loads(): lax.all_gather(wetted, 'row', axis=0, tiled=True)  59.9 us
    dot_general x6, matrix products, stiffness(): jnp.einsum('rkij,rkjn->rin', k_blocks, chosen, precision=lax.Precision.HI...  30.9 us
    gather x6, local copies, waits for them, and re-layouts, fluid_loads(): return padded_sum[return_index]  28.2 us
    all_to_all x6, starting transfers between devices, fluid_loads(): lax.all_to_all(sending, ('row', 'col'), split_axis=0, concat_axis=0, tile...  25.7 us
    gather x6, local copies, waits for them, and re-layouts, stiffness(): chosen = pieces[local_cols]  22.7 us
  transfers between devices with their start and end apart: 25, of which 7 were waited for; matrix products, arithmetic and copies ran while one was open for 20% of the time, Pallas kernels for 0%

commit v1 on v0

v1 whole, which is shorter than its diff:
```python
import functools

import jax
import jax.numpy as jnp
from jax import lax
from jax.experimental import pallas as pl
from jax.experimental.pallas import tpu as pltpu
from jax.sharding import PartitionSpec as P

DEGREE = 3
OUTER = 2
SUBLANES = 8
MESH = pl.DeviceIdType.MESH


def dot(left, right):
    return jnp.dot(left, right, preferred_element_type=jnp.float32)


def split(value):
    high = value.astype(jnp.bfloat16)
    low = (value - high.astype(jnp.float32)).astype(jnp.bfloat16)
    return high, low


def one_hot(left, right):
    return jnp.where(left == right, 1.0, 0.0).astype(jnp.bfloat16)


def kernel(
    n_row, n_col,
    rel_ref, start_ref, k_ref, send_ref, back_ref, in_ref, out_code_ref, mass_ref,
    centre_ref, inverse_ref, result_ref,
    cur, prev, v_hi, v_lo, stiff, k_hi, k_lo, pick, place, order_in, order_out,
    disp_out, disp_in, wet, partial, rs_out, rs_in, ret_out, ret_in, halo, sq_out, sq_in,
    halo_send, halo_recv, disp_send, disp_recv, wet_send, wet_recv,
    rs_send, rs_recv, ret_send, ret_recv, sq_send, sq_recv,
):
    n_dev = n_row * n_col
    my_row = lax.axis_index("row")
    my_col = lax.axis_index("col")
    me = my_row * n_col + my_col
    rows, width = cur.shape
    slots = disp_out.shape[1]
    flat = n_dev * slots
    block = k_ref.shape[2]
    pair = 2 * block
    pairs = rows // pair
    per_block = order_in.shape[0]

    def device(index):
        return (index // n_col, lax.rem(index, n_col))

    barrier = pltpu.get_barrier_semaphore()

    def greet(k, carry):
        pl.semaphore_signal(
            barrier, inc=1, device_id=device(lax.rem(me + k, n_dev)), device_id_type=MESH
        )
        return carry

    lax.fori_loop(1, n_dev, greet, 0)

    shape = (flat, rows)
    pick[...] = one_hot(send_ref[...], lax.broadcasted_iota(jnp.int32, shape, 1))
    place[...] = one_hot(lax.broadcasted_iota(jnp.int32, (rows, flat), 0), back_ref[...])
    order_in[...] = one_hot(in_ref[...], lax.broadcasted_iota(jnp.int32, (per_block, flat), 1))
    order_out[...] = one_hot(
        lax.broadcasted_iota(jnp.int32, (flat, per_block), 0), out_code_ref[...]
    )
    cur[...] = start_ref[...]
    prev[...] = start_ref[...]
    pl.semaphore_wait(barrier, n_dev - 1)

    def exchange(source, target, send, recv, k, whole):
        to = lax.rem(me + k, n_dev)
        return pltpu.make_async_remote_copy(
            src_ref=source if whole else source.at[to],
            dst_ref=target.at[me],
            send_sem=send.at[k],
            recv_sem=recv.at[k],
            device_id=device(to),
            device_id_type=MESH,
        )

    def start_all(source, target, send, recv, whole=False):
        def step(k, carry):
            exchange(source, target, send, recv, k, whole).start()
            return carry

        lax.fori_loop(1, n_dev, step, 0)

    def wait_all(source, target, send, recv, whole=False):
        def step(k, carry):
            exchange(source, target, send, recv, k, whole).wait()
            return carry

        lax.fori_loop(1, n_dev, step, 0)

    def wet_copy(k):
        return pltpu.make_async_remote_copy(
            src_ref=wet.at[my_row],
            dst_ref=wet.at[my_row],
            send_sem=wet_send.at[k],
            recv_sem=wet_recv.at[k],
            device_id=(lax.rem(my_row + k, n_row), my_col),
            device_id_type=MESH,
        )

    def rs_copy(k):
        to = lax.rem(my_col + k, n_col)
        return pltpu.make_async_remote_copy(
            src_ref=rs_out.at[to],
            dst_ref=rs_in.at[my_col],
            send_sem=rs_send.at[k],
            recv_sem=rs_recv.at[k],
            device_id=(my_row, to),
            device_id_type=MESH,
        )

    def halo_copy(side, slot):
        source = cur.at[pl.ds(rows - pair, pair)] if side == 0 else cur.at[pl.ds(0, pair)]
        to = lax.rem(me + (1 if side == 0 else n_dev - 1), n_dev)
        return pltpu.make_async_remote_copy(
            src_ref=source,
            dst_ref=halo.at[slot, side],
            send_sem=halo_send.at[side],
            recv_sem=halo_recv.at[slot, side],
            device_id=device(to),
            device_id_type=MESH,
        )

    def banded(q, first, values_hi, values_lo):
        count = values_hi.shape[0]
        window_hi = k_hi[q, :, first : first + count]
        window_lo = k_lo[q, :, first : first + count]
        return (
            dot(window_hi, values_hi) + dot(window_lo, values_hi) + dot(window_hi, values_lo)
        )

    def build_band():
        for q in range(pairs):
            for half in range(2):
                i = 2 * q + half
                for o in range(6):
                    total = jnp.zeros((block, block), jnp.float32)
                    for k in range(k_ref.shape[1]):
                        flag = (rel_ref[i, k] == o).astype(jnp.float32)
                        total = total + k_ref[i, k] * flag
                    high, low = split(total)
                    k_hi[q, half * block : (half + 1) * block, o * block : (o + 1) * block] = high
                    k_lo[q, half * block : (half + 1) * block, o * block : (o + 1) * block] = low

    def operate(step_no, degree_no):
        slot = lax.rem(step_no, 2)
        high, low = split(cur[...])
        v_hi[...] = high
        v_lo[...] = low
        chosen = dot(pick[...], v_hi[...])
        disp_out[...] = chosen.reshape(n_dev, slots, width).astype(jnp.bfloat16)
        start_all(disp_out, disp_in, disp_send, disp_recv)
        for side in range(2):
            halo_copy(side, slot).start()
        disp_in[me] = disp_out[me]

        @pl.when(step_no == 0)
        def _():
            build_band()

        for q in range(pairs):
            first = max(q - 1, 0) * pair
            last = min(q + 2, pairs) * pair
            stiff[q * pair : (q + 1) * pair, :] = banded(
                q, pair if q == 0 else 0, v_hi[first:last, :], v_lo[first:last, :]
            )
        wait_all(disp_out, disp_in, disp_send, disp_recv)
        arrived = disp_in[...].astype(jnp.float32).reshape(flat, width).astype(jnp.bfloat16)
        wet[my_row] = dot(order_in[...], arrived).astype(jnp.bfloat16)
        for k in range(1, n_row):
            wet_copy(k).start()
        for k in range(1, n_row):
            wet_copy(k).wait()
        partial[...] = dot(mass_ref[...], wet[...].reshape(n_row * per_block, width))
        rs_out[...] = partial[...].reshape(n_col, per_block, width).astype(jnp.bfloat16)
        for k in range(1, n_col):
            rs_copy(k).start()
        pressure = partial[pl.ds(pl.multiple_of(my_col * per_block, per_block), per_block), :]
        for k in range(1, n_col):
            rs_copy(k).wait()
        for k in range(1, n_col):
            pressure = pressure + rs_in[lax.rem(my_col + k, n_col)].astype(jnp.float32)
        high, low = split(pressure)
        ret_out[...] = (dot(order_out[...], high) + dot(order_out[...], low)).reshape(
            n_dev, slots, width
        )
        start_all(ret_out, ret_in, ret_send, ret_recv)
        ret_in[me] = ret_out[me]
        for side in range(2):
            halo_copy(side, slot).wait()
        high, low = split(halo[slot, 0])
        stiff[0:pair, :] += banded(0, 0, high, low)
        high, low = split(halo[slot, 1])
        stiff[rows - pair : rows, :] += banded(pairs - 1, 2 * pair, high, low)
        wait_all(ret_out, ret_in, ret_send, ret_recv)
        high, low = split(ret_in[...].reshape(flat, width))
        image = stiff[...] + (dot(place[...], high) + dot(place[...], low))
        alpha = jnp.where(degree_no == 0, 1.0, 2.0).astype(jnp.float32)
        beta = jnp.where(degree_no == 0, 0.0, 1.0).astype(jnp.float32)
        now = cur[...]
        following = (image - centre_ref[...] * now) * (alpha * inverse_ref[...]) - beta * prev[...]
        prev[...] = now
        cur[...] = following

    def filter_pass(outer_no, carry):
        def degree_step(degree_no, inner):
            operate(outer_no * DEGREE + degree_no, degree_no)
            return inner

        lax.fori_loop(0, DEGREE, degree_step, 0)
        now = cur[...]
        sq_out[...] = jnp.sum(now * now, axis=0, keepdims=True)
        target = sq_in.at[outer_no]
        start_all(sq_out, target, sq_send, sq_recv, True)
        sq_in[outer_no, me] = sq_out[...]
        wait_all(sq_out, target, sq_send, sq_recv, True)
        squares = jnp.sum(sq_in[outer_no], axis=0)
        scaled = now / jnp.sqrt(squares / (rows * n_dev) + 1e-06)
        cur[...] = scaled
        prev[...] = scaled
        return carry

    lax.fori_loop(0, OUTER, filter_pass, 0)
    result_ref[...] = cur[...]


def body(mode_block, k_blocks, block_cols, panel_node, added_mass, low_edge, high_edge):
    n_row = lax.axis_size("row")
    n_col = lax.axis_size("col")
    devices = n_row * n_col
    my_row = lax.axis_index("row")
    my_col = lax.axis_index("col")
    linear = my_row * n_col + my_col
    rows_dev, width = mode_block.shape
    block_size = k_blocks.shape[2]
    blocks_dev = rows_dev // block_size
    per_block = panel_node.shape[0] // devices
    most = 2 * ((per_block + devices - 1) // devices)
    slots = (most + SUBLANES - 1) // SUBLANES * SUBLANES
    flat = devices * slots

    panel_rows = panel_node.reshape(devices, per_block)
    source = panel_rows // rows_dev
    within = jnp.arange(per_block)
    earlier = within[None, :] < within[:, None]
    owned = source == linear
    rank = jnp.sum((owned[:, None, :] & earlier[None]).astype(jnp.int32), axis=2)
    hit = owned[:, None, :] & (rank[:, None, :] == jnp.arange(slots)[None, :, None])
    local = panel_rows - linear * rows_dev + 1
    back = jnp.sum(jnp.where(hit, local[:, None, :], 0), axis=2) - 1
    send = back.reshape(n_col, n_row, slots).transpose(1, 0, 2)

    def codes(index):
        mine = lax.dynamic_index_in_dim(source, index, 0, keepdims=False)
        same = mine[:, None] == mine[None, :]
        return mine * slots + jnp.sum((same & earlier).astype(jnp.int32), axis=1)

    in_code = codes(my_col * n_row + my_row)
    out_code = codes(linear)
    pair_base = jnp.arange(blocks_dev)[:, None] // 2 * 2
    relative = block_cols - (linear * blocks_dev - 2) - pair_base

    lower = low_edge.astype(jnp.float32) * 0.25
    upper = high_edge.astype(jnp.float32) * 0.25
    centre = (0.5 * (upper + lower)).reshape(1, width)
    inverse = (1.0 / (0.5 * (upper - lower))).reshape(1, width)

    pair = 2 * block_size
    pairs = rows_dev // pair
    f32, bf16 = jnp.float32, jnp.bfloat16
    vmem = pl.BlockSpec(memory_space=pltpu.VMEM)
    dma = pltpu.SemaphoreType.DMA
    return pl.pallas_call(
        functools.partial(kernel, n_row, n_col),
        out_shape=jax.ShapeDtypeStruct(mode_block.shape, f32),
        in_specs=[pl.BlockSpec(memory_space=pltpu.SMEM)] + [vmem] * 9,
        out_specs=vmem,
        scratch_shapes=[
            pltpu.VMEM((rows_dev, width), f32),
            pltpu.VMEM((rows_dev, width), f32),
            pltpu.VMEM((rows_dev, width), bf16),
            pltpu.VMEM((rows_dev, width), bf16),
            pltpu.VMEM((rows_dev, width), f32),
            pltpu.VMEM((pairs, pair, 3 * pair), bf16),
            pltpu.VMEM((pairs, pair, 3 * pair), bf16),
            pltpu.VMEM((flat, rows_dev), bf16),
            pltpu.VMEM((rows_dev, flat), bf16),
            pltpu.VMEM((per_block, flat), bf16),
            pltpu.VMEM((flat, per_block), bf16),
            pltpu.VMEM((devices, slots, width), bf16),
            pltpu.VMEM((devices, slots, width), bf16),
            pltpu.VMEM((n_row, per_block, width), bf16),
            pltpu.VMEM((n_col * per_block, width), f32),
            pltpu.VMEM((n_col, per_block, width), bf16),
            pltpu.VMEM((n_col, per_block, width), bf16),
            pltpu.VMEM((devices, slots, width), f32),
            pltpu.VMEM((devices, slots, width), f32),
            pltpu.VMEM((2, 2, pair, width), f32),
            pltpu.VMEM((1, width), f32),
            pltpu.VMEM((OUTER, devices, 1, width), f32),
            dma((2,)),
            dma((2, 2)),
            dma((devices,)),
            dma((devices,)),
            dma((n_row,)),
            dma((n_row,)),
            dma((n_col,)),
            dma((n_col,)),
            dma((devices,)),
            dma((devices,)),
            dma((devices,)),
            dma((devices,)),
        ],
        compiler_params=pltpu.CompilerParams(
            collective_id=0, has_side_effects=True, vmem_limit_bytes=60 * 1024 * 1024
        ),
    )(
        relative,
        mode_block,
        k_blocks,
        send.reshape(flat, 1),
        back.reshape(1, flat),
        in_code.reshape(per_block, 1),
        out_code.reshape(1, per_block),
        added_mass,
        centre,
        inverse,
    )


def solution(mesh):
    placed = (
        P(("row", "col"), None),
        P(("row", "col"), None, None, None),
        P(("row", "col"), None),
        P(),
        P("row", "col"),
        P(),
        P(),
    )
    return jax.shard_map(
        body, mesh=mesh, in_specs=placed, out_specs=P(("row", "col"), None), check_vma=False
    )
```

time: 597 us -> 243 us (0.41); the launches traced: 587 us -> 243 us
  Pallas kernels: 0 us -> 232 us
  blocking collectives: 209 us -> 0 us
  local copies, waits for them, and re-layouts: 123 us -> 5.19 us
  waiting for transfers between devices: 106 us -> 0 us
  starting transfers between devices: 53.9 us -> 0 us
  matrix products: 38.6 us -> 0 us
  other arithmetic: 42.1 us -> 5.61 us
  between operations: 14.3 us -> 0.06 us
    pallas_call x0 -> x1, Pallas kernels: none -> 232 us  [body(): pl.pallas_call(functools.partial(kernel, n_row, n_col), out_shape=jax.Sha...]
    reduce_scatter x6 -> x0, waiting for transfers between devices: 105 us -> none  [fluid_loads(): lax.psum_scatter(partial_value, 'col', scatter_dimension=0, tiled=True)]
    psum x2 -> x0, blocking collectives: 80.9 us -> none  [body(): squares = lax.psum(jnp.sum(current * current, axis=0), ('row', 'col'))]
    gather x30 -> x0, local copies, waits for them, and re-layouts: 73.5 us -> none  [the longest x6 28.2 us: fluid_loads(): return padded_sum[return_index]]
    all_to_all x5 -> x0, blocking collectives: 68.7 us -> none  [fluid_loads(): lax.all_to_all(outgoing.reshape(devices, slot_count, mode_width), ('row',...]
    all_gather x6 -> x0, blocking collectives: 59.9 us -> none  [fluid_loads(): lax.all_gather(wetted, 'row', axis=0, tiled=True)]
    dot_general x12 -> x0, matrix products: 38.6 us -> none  [the longest x6 30.9 us: stiffness(): jnp.einsum('rkij,rkjn->rin', k_blocks, chosen, precision=lax.Precision.HI...]
    all_to_all x7 -> x0, starting transfers between devices: 33 us -> none  [the longest x6 25.7 us: fluid_loads(): lax.all_to_all(sending, ('row', 'col'), split_axis=0, concat_axis=0, tile...]
  transfers between devices with their start and end apart: 25 -> 0, of which waited for: 7 -> 0; matrix products, arithmetic and copies ran while one was open for 20% -> 0% of each run, Pallas kernels for 0% -> 0%
where the time goes in v1:
time: 243 us
  Pallas kernels  232 us (95%)
  other arithmetic  5.61 us (2%)
  local copies, waits for them, and re-layouts  5.19 us (2%)
    pallas_call x1, Pallas kernels, body(): pl.pallas_call(functools.partial(kernel, n_row, n_col), out_shape=jax.Sha...  232 us

profile of v1, /device:TPU:0, one launch (start us, length us, event | category | flops | bytes accessed | tf_op | source)
XLA Modules:
  0.0 242.6 jit_solution(5018183587523670344)
XLA Ops:
  0.0 1.3 multiply_divide_fusion
  1.3 0.7 broadcast_compare_fusion
  2.0 0.8 copy.22
  2.8 0.7 subtract_subtract_fusion.rel_ref
  3.5 0.6 convert_reduce_fusion
  4.1 0.7 add_select_fusion
  4.8 0.6 select_reduce_fusion
  5.5 0.2 convert_reduce_fusion.1
  5.6 0.6 bitcast_add_fusion
  6.2 0.2 convert_reduce_fusion.2
  6.4 0.7 sub.59.back_ref
  7.1 0.7 copy.25.in_ref
  7.8 0.8 reshape.146.send_ref
  8.6 231.7 %shard_map.73 = f32[1024,256]{1,0:T(8,128)} custom-call(s32[8,3]{1,0:T(8,128)} %subtract_subtract_fusion.rel_ref, f32[1024,256]{1,0:T(8,128)} %start_ref.1, f32[8,3,128,128]{3,2,1,0:T(8,128)} %k_ref.1, s32[256,1]{1,0:T(8,128)} %reshape.146.send_ref, s32[1,256]{1,0:T(1,128)} %sub.59.back_ref, s32[128,1]{1,0:T(8,128)} %copy.25.in_ref, ...), custom_call_target="tpu_custom_call" | custom-call | tf_op jit(solution)/shard_map/pallas_call | solution.py:282
  240.3 2.3 copy.29
  (6 shorter events, 0.1 us)

commit v2 on v1

--- a/solution.py
+++ b/solution.py
@@ -10,6 +10,8 @@
 DEGREE = 3
 OUTER = 2
 SUBLANES = 8
+PACKED = 16
+CODE_BITS = 15.0
 MESH = pl.DeviceIdType.MESH
 
 
@@ -21,6 +23,19 @@
     high = value.astype(jnp.bfloat16)
     low = (value - high.astype(jnp.float32)).astype(jnp.bfloat16)
     return high, low
+
+
+def encode(value):
+    largest = jnp.maximum(jnp.max(jnp.abs(value), axis=0, keepdims=True), 1e-30)
+    power = jnp.ceil(jnp.log2(largest))
+    coded = jnp.clip(jnp.round(value * jnp.exp2(CODE_BITS - power)), -32767.0, 32767.0)
+    powers = jnp.broadcast_to(power, (PACKED, value.shape[1]))
+    return coded.astype(jnp.int32).astype(jnp.int16), powers.astype(jnp.int32).astype(jnp.int16)
+
+
+def decode(coded, powers):
+    power = powers.astype(jnp.int32).astype(jnp.float32)[0:1]
+    return coded.astype(jnp.int32).astype(jnp.float32) * jnp.exp2(power - CODE_BITS)
 
 
 def one_hot(left, right):
@@ -32,7 +47,7 @@
     rel_ref, start_ref, k_ref, send_ref, back_ref, in_ref, out_code_ref, mass_ref,
     centre_ref, inverse_ref, result_ref,
     cur, prev, v_hi, v_lo, stiff, k_hi, k_lo, pick, place, order_in, order_out,
-    disp_out, disp_in, wet, partial, rs_out, rs_in, ret_out, ret_in, halo, sq_out, sq_in,
+    disp_out, disp_in, wet, partial, rs_out, rs_in, ret_out, ret_in, halo_out, halo, sq_out, sq_in,
     halo_send, halo_recv, disp_send, disp_recv, wet_send, wet_recv,
     rs_send, rs_recv, ret_send, ret_recv, sq_send, sq_recv,
 ):
@@ -97,13 +112,27 @@
 
         lax.fori_loop(1, n_dev, step, 0)
 
+    chips = n_row // 2
+    partner = my_row + 1 - 2 * lax.rem(my_row, 2)
+
     def wet_copy(k):
         return pltpu.make_async_remote_copy(
             src_ref=wet.at[my_row],
             dst_ref=wet.at[my_row],
             send_sem=wet_send.at[k],
             recv_sem=wet_recv.at[k],
-            device_id=(lax.rem(my_row + k, n_row), my_col),
+            device_id=(lax.rem(my_row + 2 * k, n_row), my_col),
+            device_id_type=MESH,
+        )
+
+    def wet_forward(k):
+        held = wet.at[lax.rem(my_row + n_row - 2 * k, n_row)]
+        return pltpu.make_async_remote_copy(
+            src_ref=held,
+            dst_ref=held,
+            send_sem=wet_send.at[chips + k],
+            recv_sem=wet_recv.at[chips + k],
+            device_id=(partner, my_col),
             device_id_type=MESH,
         )
 
@@ -119,10 +148,9 @@
         )
 
     def halo_copy(side, slot):
-        source = cur.at[pl.ds(rows - pair, pair)] if side == 0 else cur.at[pl.ds(0, pair)]
         to = lax.rem(me + (1 if side == 0 else n_dev - 1), n_dev)
         return pltpu.make_async_remote_copy(
-            src_ref=source,
+            src_ref=halo_out.at[side],
             dst_ref=halo.at[slot, side],
             send_sem=halo_send.at[side],
             recv_sem=halo_recv.at[slot, side],
@@ -160,7 +188,10 @@
         disp_out[...] = chosen.reshape(n_dev, slots, width).astype(jnp.bfloat16)
         start_all(disp_out, disp_in, disp_send, disp_recv)
         for side in range(2):
-            halo_copy(side, slot).start()
+            edge = cur[rows - pair : rows, :] if side == 0 else cur[0:pair, :]
+            coded, powers = encode(edge)
+            halo_out[side, 0:pair, :] = coded
+            halo_out[side, pair : pair + PACKED, :] = powers
         disp_in[me] = disp_out[me]
 
         @pl.when(step_no == 0)
@@ -176,34 +207,46 @@
         wait_all(disp_out, disp_in, disp_send, disp_recv)
         arrived = disp_in[...].astype(jnp.float32).reshape(flat, width).astype(jnp.bfloat16)
         wet[my_row] = dot(order_in[...], arrived).astype(jnp.bfloat16)
-        for k in range(1, n_row):
+        for k in range(1, chips):
             wet_copy(k).start()
-        for k in range(1, n_row):
-            wet_copy(k).wait()
+        wet_forward(0).start()
+        for side in range(2):
+            halo_copy(side, slot).start()
+        for k in range(1, chips):
+            wet_copy(k).wait_recv()
+            wet_forward(k).start()
+        for k in range(1, chips):
+            wet_copy(k).wait_send()
+        for k in range(chips):
+            wet_forward(k).wait()
         partial[...] = dot(mass_ref[...], wet[...].reshape(n_row * per_block, width))
-        rs_out[...] = partial[...].reshape(n_col, per_block, width).astype(jnp.bfloat16)
+        coded, powers = encode(partial[...])
+        for j in range(n_col):
+            rs_out[j, 0:per_block, :] = coded[j * per_block : (j + 1) * per_block, :]
+            rs_out[j, per_block : per_block + PACKED, :] = powers
         for k in range(1, n_col):
             rs_copy(k).start()
         pressure = partial[pl.ds(pl.multiple_of(my_col * per_block, per_block), per_block), :]
         for k in range(1, n_col):
             rs_copy(k).wait()
         for k in range(1, n_col):
-            pressure = pressure + rs_in[lax.rem(my_col + k, n_col)].astype(jnp.float32)
-        high, low = split(pressure)
-        ret_out[...] = (dot(order_out[...], high) + dot(order_out[...], low)).reshape(
-            n_dev, slots, width
-        )
+            other = lax.rem(my_col + k, n_col)
+            pressure = pressure + decode(
+                rs_in[other, 0:per_block, :], rs_in[other, per_block : per_block + PACKED, :]
+            )
+        ordered = dot(order_out[...], pressure.astype(jnp.bfloat16))
+        ret_out[...] = ordered.reshape(n_dev, slots, width).astype(jnp.bfloat16)
         start_all(ret_out, ret_in, ret_send, ret_recv)
         ret_in[me] = ret_out[me]
         for side in range(2):
             halo_copy(side, slot).wait()
-        high, low = split(halo[slot, 0])
+        high, low = split(decode(halo[slot, 0, 0:pair, :], halo[slot, 0, pair : pair + PACKED, :]))
         stiff[0:pair, :] += banded(0, 0, high, low)
-        high, low = split(halo[slot, 1])
+        high, low = split(decode(halo[slot, 1, 0:pair, :], halo[slot, 1, pair : pair + PACKED, :]))
         stiff[rows - pair : rows, :] += banded(pairs - 1, 2 * pair, high, low)
         wait_all(ret_out, ret_in, ret_send, ret_recv)
-        high, low = split(ret_in[...].reshape(flat, width))
-        image = stiff[...] + (dot(place[...], high) + dot(place[...], low))
+        returned = ret_in[...].astype(jnp.float32).reshape(flat, width).astype(jnp.bfloat16)
+        image = stiff[...] + dot(place[...], returned)
         alpha = jnp.where(degree_no == 0, 1.0, 2.0).astype(jnp.float32)
         beta = jnp.where(degree_no == 0, 0.0, 1.0).astype(jnp.float32)
         now = cur[...]
@@ -300,11 +343,12 @@
             pltpu.VMEM((devices, slots, width), bf16),
             pltpu.VMEM((n_row, per_block, width), bf16),
             pltpu.VMEM((n_col * per_block, width), f32),
-            pltpu.VMEM((n_col, per_block, width), bf16),
-            pltpu.VMEM((n_col, per_block, width), bf16),
-            pltpu.VMEM((devices, slots, width), f32),
-            pltpu.VMEM((devices, slots, width), f32),
-            pltpu.VMEM((2, 2, pair, width), f32),
+            pltpu.VMEM((n_col, per_block + PACKED, width), jnp.int16),
+            pltpu.VMEM((n_col, per_block + PACKED, width), jnp.int16),
+            pltpu.VMEM((devices, slots, width), bf16),
+            pltpu.VMEM((devices, slots, width), bf16),
+            pltpu.VMEM((2, pair + PACKED, width), jnp.int16),
+            pltpu.VMEM((2, 2, pair + PACKED, width), jnp.int16),
             pltpu.VMEM((1, width), f32),
             pltpu.VMEM((OUTER, devices, 1, width), f32),
             dma((2,)),

time: 243 us -> 196 us (0.81)
  Pallas kernels: 232 us -> 185 us
    pallas_call x1, Pallas kernels: 232 us -> 185 us  [body(): pl.pallas_call(functools.partial(kernel, n_row, n_col), out_shape=jax.Sha...]
where the time goes in v2:
time: 196 us
  Pallas kernels  185 us (94%)
  other arithmetic  5.61 us (3%)
  local copies, waits for them, and re-layouts  5.19 us (3%)
    pallas_call x1, Pallas kernels, body(): pl.pallas_call(functools.partial(kernel, n_row, n_col), out_shape=jax.Sha...  185 us

profile of v2, /device:TPU:0, one launch (start us, length us, event | category | flops | bytes accessed | tf_op | source)
XLA Modules:
  0.0 196.0 jit_solution(2397365219423875168)
XLA Ops:
  0.0 1.3 multiply_divide_fusion
  1.3 0.7 broadcast_compare_fusion
  2.0 0.8 copy.22
  2.8 0.7 subtract_subtract_fusion.rel_ref
  3.5 0.6 convert_reduce_fusion
  4.1 0.7 add_select_fusion
  4.8 0.6 select_reduce_fusion
  5.5 0.2 convert_reduce_fusion.1
  5.6 0.6 bitcast_add_fusion
  6.2 0.2 convert_reduce_fusion.2
  6.4 0.7 sub.59.back_ref
  7.1 0.7 copy.25.in_ref
  7.8 0.8 reshape.146.send_ref
  8.6 185.1 %shard_map.73 = f32[1024,256]{1,0:T(8,128)} custom-call(s32[8,3]{1,0:T(8,128)} %subtract_subtract_fusion.rel_ref, f32[1024,256]{1,0:T(8,128)} %start_ref.1, f32[8,3,128,128]{3,2,1,0:T(8,128)} %k_ref.1, s32[256,1]{1,0:T(8,128)} %reshape.146.send_ref, s32[1,256]{1,0:T(1,128)} %sub.59.back_ref, s32[128,1]{1,0:T(8,128)} %copy.25.in_ref, ...), custom_call_target="tpu_custom_call" | custom-call | tf_op jit(solution)/shard_map/pallas_call | solution.py:325
  193.7 2.3 %copy.29 = f32[1024,256]{1,0:T(8,128)} copy(f32[1024,256]{1,0:T(8,128)} %shard_map.73) | data formatting | bytes 2097152
  (6 shorter events, 0.1 us)

commit v3 on v2

v3 whole, which is shorter than its diff:
```python
import functools

import jax
import jax.numpy as jnp
from jax import lax
from jax.experimental import pallas as pl
from jax.experimental.pallas import tpu as pltpu
from jax.sharding import PartitionSpec as P

DEGREE = 3
OUTER = 2
SUBLANES = 8
PACKED = 16
CODE_BITS = 15.0
CHAINS = 2
MESH = pl.DeviceIdType.MESH


def dot(left, right):
    return jnp.dot(left, right, preferred_element_type=jnp.float32)


def split(value):
    high = value.astype(jnp.bfloat16)
    low = (value - high.astype(jnp.float32)).astype(jnp.bfloat16)
    return high, low


def encode(value):
    largest = jnp.maximum(jnp.max(jnp.abs(value), axis=0, keepdims=True), 1e-30)
    power = jnp.ceil(jnp.log2(largest))
    coded = jnp.clip(jnp.round(value * jnp.exp2(CODE_BITS - power)), -32767.0, 32767.0)
    powers = jnp.broadcast_to(power, (PACKED, value.shape[1]))
    return coded.astype(jnp.int32).astype(jnp.int16), powers.astype(jnp.int32).astype(jnp.int16)


def decode(coded, powers):
    power = powers.astype(jnp.int32).astype(jnp.float32)[0:1]
    return coded.astype(jnp.int32).astype(jnp.float32) * jnp.exp2(power - CODE_BITS)


def one_hot(left, right):
    return jnp.where(left == right, 1.0, 0.0).astype(jnp.bfloat16)


def kernel(
    n_row, n_col,
    rel_ref, start_ref, k_ref, send_ref, back_ref, in_ref, out_code_ref, mass_ref,
    centre_ref, inverse_ref, result_ref,
    cur, prev, v_hi, v_lo, stiff, k_hi, k_lo, pick, place, order_in, order_out,
    disp_out, disp_in, wet, partial, rs_out, rs_in, ret_out, ret_in, halo_out, halo, sq_out, sq_in,
    halo_send, halo_recv, disp_send, disp_recv, wet_send, wet_recv,
    rs_send, rs_recv, ret_send, ret_recv, sq_send, sq_recv,
):
    n_dev = n_row * n_col
    my_row = lax.axis_index("row")
    my_col = lax.axis_index("col")
    me = my_row * n_col + my_col
    chains, rows, width = cur.shape
    slots = disp_out.shape[2]
    flat = n_dev * slots
    block = k_ref.shape[2]
    pair = 2 * block
    pairs = rows // pair
    per_block = order_in.shape[0]

    def device(index):
        return (index // n_col, lax.rem(index, n_col))

    barrier = pltpu.get_barrier_semaphore()

    def greet(k, carry):
        pl.semaphore_signal(
            barrier, inc=1, device_id=device(lax.rem(me + k, n_dev)), device_id_type=MESH
        )
        return carry

    lax.fori_loop(1, n_dev, greet, 0)

    shape = (flat, rows)
    pick[...] = one_hot(send_ref[...], lax.broadcasted_iota(jnp.int32, shape, 1))
    place[...] = one_hot(lax.broadcasted_iota(jnp.int32, (rows, flat), 0), back_ref[...])
    order_in[...] = one_hot(in_ref[...], lax.broadcasted_iota(jnp.int32, (per_block, flat), 1))
    order_out[...] = one_hot(
        lax.broadcasted_iota(jnp.int32, (flat, per_block), 0), out_code_ref[...]
    )
    for h in range(chains):
        cur[h] = start_ref[:, h * width : (h + 1) * width]
        prev[h] = start_ref[:, h * width : (h + 1) * width]
    pl.semaphore_wait(barrier, n_dev - 1)

    def exchange(source, target, send, recv, h, k, whole):
        to = lax.rem(me + k, n_dev)
        return pltpu.make_async_remote_copy(
            src_ref=source if whole else source.at[to],
            dst_ref=target.at[me],
            send_sem=send.at[h, k],
            recv_sem=recv.at[h, k],
            device_id=device(to),
            device_id_type=MESH,
        )

    def start_all(source, target, send, recv, h, whole=False):
        def step(k, carry):
            exchange(source, target, send, recv, h, k, whole).start()
            return carry

        lax.fori_loop(1, n_dev, step, 0)

    def wait_all(source, target, send, recv, h, whole=False):
        def step(k, carry):
            exchange(source, target, send, recv, h, k, whole).wait()
            return carry

        lax.fori_loop(1, n_dev, step, 0)

    chips = n_row // 2
    partner = my_row + 1 - 2 * lax.rem(my_row, 2)

    def wet_copy(h, k):
        return pltpu.make_async_remote_copy(
            src_ref=wet.at[h, my_row],
            dst_ref=wet.at[h, my_row],
            send_sem=wet_send.at[h, k],
            recv_sem=wet_recv.at[h, k],
            device_id=(lax.rem(my_row + 2 * k, n_row), my_col),
            device_id_type=MESH,
        )

    def wet_forward(h, k):
        held = wet.at[h, lax.rem(my_row + n_row - 2 * k, n_row)]
        return pltpu.make_async_remote_copy(
            src_ref=held,
            dst_ref=held,
            send_sem=wet_send.at[h, chips + k],
            recv_sem=wet_recv.at[h, chips + k],
            device_id=(partner, my_col),
            device_id_type=MESH,
        )

    def rs_copy(h, k):
        to = lax.rem(my_col + k, n_col)
        return pltpu.make_async_remote_copy(
            src_ref=rs_out.at[h, to],
            dst_ref=rs_in.at[h, my_col],
            send_sem=rs_send.at[h, k],
            recv_sem=rs_recv.at[h, k],
            device_id=(my_row, to),
            device_id_type=MESH,
        )

    def halo_copy(h, side, slot):
        to = lax.rem(me + (1 if side == 0 else n_dev - 1), n_dev)
        return pltpu.make_async_remote_copy(
            src_ref=halo_out.at[h, side],
            dst_ref=halo.at[h, slot, side],
            send_sem=halo_send.at[h, side],
            recv_sem=halo_recv.at[h, slot, side],
            device_id=device(to),
            device_id_type=MESH,
        )

    def banded(q, first, values_hi, values_lo):
        count = values_hi.shape[0]
        window_hi = k_hi[q, :, first : first + count]
        window_lo = k_lo[q, :, first : first + count]
        return (
            dot(window_hi, values_hi) + dot(window_lo, values_hi) + dot(window_hi, values_lo)
        )

    def build_band():
        for q in range(pairs):
            for half in range(2):
                i = 2 * q + half
                for o in range(6):
                    total = jnp.zeros((block, block), jnp.float32)
                    for k in range(k_ref.shape[1]):
                        flag = (rel_ref[i, k] == o).astype(jnp.float32)
                        total = total + k_ref[i, k] * flag
                    high, low = split(total)
                    k_hi[q, half * block : (half + 1) * block, o * block : (o + 1) * block] = high
                    k_lo[q, half * block : (half + 1) * block, o * block : (o + 1) * block] = low

    def columns(h):
        return slice(h * width, (h + 1) * width)

    def rescale(h, outer_no):
        wait_all(sq_out.at[h], sq_in.at[h, outer_no], sq_send, sq_recv, h, True)
        squares = jnp.sum(sq_in[h, outer_no], axis=0)
        scaled = cur[h] / jnp.sqrt(squares / (rows * n_dev) + 1e-06)
        cur[h] = scaled
        prev[h] = scaled

    def dispatch(h, step_no):
        @pl.when((step_no > 0) & (lax.rem(step_no, DEGREE) == 0))
        def _():
            rescale(h, step_no // DEGREE - 1)

        high, low = split(cur[h])
        v_hi[h] = high
        v_lo[h] = low
        chosen = dot(pick[...], v_hi[h])
        disp_out[h] = chosen.reshape(n_dev, slots, width).astype(jnp.bfloat16)
        start_all(disp_out.at[h], disp_in.at[h], disp_send, disp_recv, h)
        for side in range(2):
            edge = cur[h, rows - pair : rows, :] if side == 0 else cur[h, 0:pair, :]
            coded, powers = encode(edge)
            halo_out[h, side, 0:pair, :] = coded
            halo_out[h, side, pair : pair + PACKED, :] = powers
        disp_in[h, me] = disp_out[h, me]
        if h == 0:
            @pl.when(step_no == 0)
            def _():
                build_band()

        for q in range(pairs):
            first = max(q - 1, 0) * pair
            last = min(q + 2, pairs) * pair
            stiff[h, q * pair : (q + 1) * pair, :] = banded(
                q, pair if q == 0 else 0, v_hi[h, first:last, :], v_lo[h, first:last, :]
            )

    def gather(h, step_no):
        wait_all(disp_out.at[h], disp_in.at[h], disp_send, disp_recv, h)
        arrived = disp_in[h].astype(jnp.float32).reshape(flat, width).astype(jnp.bfloat16)
        wet[h, my_row] = dot(order_in[...], arrived).astype(jnp.bfloat16)
        for k in range(1, chips):
            wet_copy(h, k).start()
        wet_forward(h, 0).start()
        for side in range(2):
            halo_copy(h, side, lax.rem(step_no, 2)).start()

    def multiply(h, step_no):
        for k in range(1, chips):
            wet_copy(h, k).wait_recv()
            wet_forward(h, k).start()
        for k in range(1, chips):
            wet_copy(h, k).wait_send()
        for k in range(chips):
            wet_forward(h, k).wait()
        partial[h] = dot(mass_ref[...], wet[h].reshape(n_row * per_block, width))
        coded, powers = encode(partial[h])
        for j in range(n_col):
            rs_out[h, j, 0:per_block, :] = coded[j * per_block : (j + 1) * per_block, :]
            rs_out[h, j, per_block : per_block + PACKED, :] = powers
        for k in range(1, n_col):
            rs_copy(h, k).start()

    def give_back(h, step_no):
        own = pl.ds(pl.multiple_of(my_col * per_block, per_block), per_block)
        pressure = partial[h, own, :]
        for k in range(1, n_col):
            rs_copy(h, k).wait()
        for k in range(1, n_col):
            other = lax.rem(my_col + k, n_col)
            pressure = pressure + decode(
                rs_in[h, other, 0:per_block, :], rs_in[h, other, per_block : per_block + PACKED, :]
            )
        ordered = dot(order_out[...], pressure.astype(jnp.bfloat16))
        ret_out[h] = ordered.reshape(n_dev, slots, width).astype(jnp.bfloat16)
        start_all(ret_out.at[h], ret_in.at[h], ret_send, ret_recv, h)
        ret_in[h, me] = ret_out[h, me]
        slot = lax.rem(step_no, 2)
        for side in range(2):
            halo_copy(h, side, slot).wait()
            edge = decode(halo[h, slot, side, 0:pair, :], halo[h, slot, side, pair : pair + PACKED, :])
            high, low = split(edge)
            if side == 0:
                stiff[h, 0:pair, :] += banded(0, 0, high, low)
            else:
                stiff[h, rows - pair : rows, :] += banded(pairs - 1, 2 * pair, high, low)

    def update(h, step_no):
        wait_all(ret_out.at[h], ret_in.at[h], ret_send, ret_recv, h)
        returned = ret_in[h].astype(jnp.float32).reshape(flat, width).astype(jnp.bfloat16)
        image = stiff[h] + dot(place[...], returned)
        degree_no = lax.rem(step_no, DEGREE)
        alpha = jnp.where(degree_no == 0, 1.0, 2.0).astype(jnp.float32)
        beta = jnp.where(degree_no == 0, 0.0, 1.0).astype(jnp.float32)
        now = cur[h]
        inverse = inverse_ref[:, columns(h)]
        following = (image - centre_ref[:, columns(h)] * now) * (alpha * inverse) - beta * prev[h]
        prev[h] = now
        cur[h] = following

        @pl.when(degree_no == DEGREE - 1)
        def _():
            sq_out[h] = jnp.sum(following * following, axis=0, keepdims=True)
            outer_no = step_no // DEGREE
            start_all(sq_out.at[h], sq_in.at[h, outer_no], sq_send, sq_recv, h, True)
            sq_in[h, outer_no, me] = sq_out[h]

    steps = OUTER * DEGREE

    def both(step_no, carry):
        late = step_no - 1
        dispatch(0, step_no)

        @pl.when(step_no > 0)
        def _():
            give_back(1, late)

        gather(0, step_no)

        @pl.when(step_no > 0)
        def _():
            update(1, late)

        multiply(0, step_no)
        dispatch(1, step_no)
        give_back(0, step_no)
        gather(1, step_no)
        update(0, step_no)
        multiply(1, step_no)
        return carry

    lax.fori_loop(0, steps, both, 0)
    give_back(1, steps - 1)
    rescale(0, OUTER - 1)
    update(1, steps - 1)
    result_ref[:, columns(0)] = cur[0]
    rescale(1, OUTER - 1)
    result_ref[:, columns(1)] = cur[1]


def body(mode_block, k_blocks, block_cols, panel_node, added_mass, low_edge, high_edge):
    n_row = lax.axis_size("row")
    n_col = lax.axis_size("col")
    devices = n_row * n_col
    my_row = lax.axis_index("row")
    my_col = lax.axis_index("col")
    linear = my_row * n_col + my_col
    rows_dev, width = mode_block.shape
    block_size = k_blocks.shape[2]
    blocks_dev = rows_dev // block_size
    per_block = panel_node.shape[0] // devices
    most = 2 * ((per_block + devices - 1) // devices)
    slots = (most + SUBLANES - 1) // SUBLANES * SUBLANES
    flat = devices * slots

    panel_rows = panel_node.reshape(devices, per_block)
    source = panel_rows // rows_dev
    within = jnp.arange(per_block)
    earlier = within[None, :] < within[:, None]
    owned = source == linear
    rank = jnp.sum((owned[:, None, :] & earlier[None]).astype(jnp.int32), axis=2)
    hit = owned[:, None, :] & (rank[:, None, :] == jnp.arange(slots)[None, :, None])
    local = panel_rows - linear * rows_dev + 1
    back = jnp.sum(jnp.where(hit, local[:, None, :], 0), axis=2) - 1
    send = back.reshape(n_col, n_row, slots).transpose(1, 0, 2)

    def codes(index):
        mine = lax.dynamic_index_in_dim(source, index, 0, keepdims=False)
        same = mine[:, None] == mine[None, :]
        return mine * slots + jnp.sum((same & earlier).astype(jnp.int32), axis=1)

    in_code = codes(my_col * n_row + my_row)
    out_code = codes(linear)
    pair_base = jnp.arange(blocks_dev)[:, None] // 2 * 2
    relative = block_cols - (linear * blocks_dev - 2) - pair_base

    lower = low_edge.astype(jnp.float32) * 0.25
    upper = high_edge.astype(jnp.float32) * 0.25
    centre = (0.5 * (upper + lower)).reshape(1, width)
    inverse = (1.0 / (0.5 * (upper - lower))).reshape(1, width)

    pair = 2 * block_size
    pairs = rows_dev // pair
    f32, bf16 = jnp.float32, jnp.bfloat16
    vmem = pl.BlockSpec(memory_space=pltpu.VMEM)
    part = width // CHAINS
    dma = pltpu.SemaphoreType.DMA
    return pl.pallas_call(
        functools.partial(kernel, n_row, n_col),
        out_shape=jax.ShapeDtypeStruct(mode_block.shape, f32),
        in_specs=[pl.BlockSpec(memory_space=pltpu.SMEM)] + [vmem] * 9,
        out_specs=vmem,
        scratch_shapes=[
            pltpu.VMEM((CHAINS, rows_dev, part), f32),
            pltpu.VMEM((CHAINS, rows_dev, part), f32),
            pltpu.VMEM((CHAINS, rows_dev, part), bf16),
            pltpu.VMEM((CHAINS, rows_dev, part), bf16),
            pltpu.VMEM((CHAINS, rows_dev, part), f32),
            pltpu.VMEM((pairs, pair, 3 * pair), bf16),
            pltpu.VMEM((pairs, pair, 3 * pair), bf16),
            pltpu.VMEM((flat, rows_dev), bf16),
            pltpu.VMEM((rows_dev, flat), bf16),
            pltpu.VMEM((per_block, flat), bf16),
            pltpu.VMEM((flat, per_block), bf16),
            pltpu.VMEM((CHAINS, devices, slots, part), bf16),
            pltpu.VMEM((CHAINS, devices, slots, part), bf16),
            pltpu.VMEM((CHAINS, n_row, per_block, part), bf16),
            pltpu.VMEM((CHAINS, n_col * per_block, part), f32),
            pltpu.VMEM((CHAINS, n_col, per_block + PACKED, part), jnp.int16),
            pltpu.VMEM((CHAINS, n_col, per_block + PACKED, part), jnp.int16),
            pltpu.VMEM((CHAINS, devices, slots, part), bf16),
            pltpu.VMEM((CHAINS, devices, slots, part), bf16),
            pltpu.VMEM((CHAINS, 2, pair + PACKED, part), jnp.int16),
            pltpu.VMEM((CHAINS, 2, 2, pair + PACKED, part), jnp.int16),
            pltpu.VMEM((CHAINS, 1, part), f32),
            pltpu.VMEM((CHAINS, OUTER, devices, 1, part), f32),
            dma((CHAINS, 2)),
            dma((CHAINS, 2, 2)),
            dma((CHAINS, devices)),
            dma((CHAINS, devices)),
            dma((CHAINS, n_row)),
            dma((CHAINS, n_row)),
            dma((CHAINS, n_col)),
            dma((CHAINS, n_col)),
            dma((CHAINS, devices)),
            dma((CHAINS, devices)),
            dma((CHAINS, devices)),
            dma((CHAINS, devices)),
        ],
        compiler_params=pltpu.CompilerParams(
            collective_id=0, has_side_effects=True, vmem_limit_bytes=60 * 1024 * 1024
        ),
    )(
        relative,
        mode_block,
        k_blocks,
        send.reshape(flat, 1),
        back.reshape(1, flat),
        in_code.reshape(per_block, 1),
        out_code.reshape(1, per_block),
        added_mass,
        centre,
        inverse,
    )


def solution(mesh):
    placed = (
        P(("row", "col"), None),
        P(("row", "col"), None, None, None),
        P(("row", "col"), None),
        P(),
        P("row", "col"),
        P(),
        P(),
    )
    return jax.shard_map(
        body, mesh=mesh, in_specs=placed, out_specs=P(("row", "col"), None), check_vma=False
    )
```

time: 196 us -> 198 us (1.010)
  no operation moved by 1% of the time
where the time goes in v3:
time: 198 us; the launch traced here: 197 us
  Pallas kernels  186 us (94%)
  other arithmetic  5.61 us (3%)
  local copies, waits for them, and re-layouts  5.19 us (3%)
    pallas_call x1, Pallas kernels, body(): pl.pallas_call(functools.partial(kernel, n_row, n_col), out_shape=jax.Sha...  186 us

profile of v3, /device:TPU:0, one launch (start us, length us, event | category | flops | bytes accessed | tf_op | source)
XLA Modules:
  0.0 197.4 jit_solution(16700147029332269013)
XLA Ops:
  0.0 1.3 multiply_divide_fusion
  1.3 0.7 broadcast_compare_fusion
  2.0 0.8 copy.22
  2.8 0.7 subtract_subtract_fusion.rel_ref
  3.5 0.6 convert_reduce_fusion
  4.1 0.7 add_select_fusion
  4.8 0.6 select_reduce_fusion
  5.5 0.2 convert_reduce_fusion.1
  5.6 0.6 bitcast_add_fusion
  6.2 0.2 convert_reduce_fusion.2
  6.4 0.7 sub.59.back_ref
  7.1 0.7 copy.25.in_ref
  7.8 0.8 reshape.146.send_ref
  8.6 186.5 %shard_map.73 = f32[1024,256]{1,0:T(8,128)} custom-call(s32[8,3]{1,0:T(8,128)} %subtract_subtract_fusion.rel_ref, f32[1024,256]{1,0:T(8,128)} %start_ref.1, f32[8,3,128,128]{3,2,1,0:T(8,128)} %k_ref.1, s32[256,1]{1,0:T(8,128)} %reshape.146.send_ref, s32[1,256]{1,0:T(1,128)} %sub.59.back_ref, s32[128,1]{1,0:T(8,128)} %copy.25.in_ref, ...), custom_call_target="tpu_custom_call" | custom-call | tf_op jit(solution)/shard_map/pallas_call | solution.py:373
  195.1 2.3 %copy.29 = f32[1024,256]{1,0:T(8,128)} copy(f32[1024,256]{1,0:T(8,128)} %shard_map.73) | data formatting | bytes 2097152
  (6 shorter events, 0.1 us)

commit v4 on v2

--- a/solution.py
+++ b/solution.py
@@ -47,7 +47,7 @@
     rel_ref, start_ref, k_ref, send_ref, back_ref, in_ref, out_code_ref, mass_ref,
     centre_ref, inverse_ref, result_ref,
     cur, prev, v_hi, v_lo, stiff, k_hi, k_lo, pick, place, order_in, order_out,
-    disp_out, disp_in, wet, partial, rs_out, rs_in, ret_out, ret_in, halo_out, halo, sq_out, sq_in,
+    disp_out, disp_in, wet, rs_out, rs_in, ret_out, ret_in, halo_out, halo, sq_out, sq_in,
     halo_send, halo_recv, disp_send, disp_recv, wet_send, wet_recv,
     rs_send, rs_recv, ret_send, ret_recv, sq_send, sq_recv,
 ):
@@ -219,14 +219,19 @@
             wet_copy(k).wait_send()
         for k in range(chips):
             wet_forward(k).wait()
-        partial[...] = dot(mass_ref[...], wet[...].reshape(n_row * per_block, width))
-        coded, powers = encode(partial[...])
-        for j in range(n_col):
-            rs_out[j, 0:per_block, :] = coded[j * per_block : (j + 1) * per_block, :]
-            rs_out[j, per_block : per_block + PACKED, :] = powers
+        gathered = wet[...].reshape(n_row * per_block, width)
+
+        def product(index):
+            chunk = pl.ds(pl.multiple_of(index * per_block, per_block), per_block)
+            return dot(mass_ref[chunk, :], gathered)
+
         for k in range(1, n_col):
+            other = lax.rem(my_col + k, n_col)
+            coded, powers = encode(product(other))
+            rs_out[other, 0:per_block, :] = coded
+            rs_out[other, per_block : per_block + PACKED, :] = powers
             rs_copy(k).start()
-        pressure = partial[pl.ds(pl.multiple_of(my_col * per_block, per_block), per_block), :]
+        pressure = product(my_col)
         for k in range(1, n_col):
             rs_copy(k).wait()
         for k in range(1, n_col):
@@ -342,7 +347,6 @@
             pltpu.VMEM((devices, slots, width), bf16),
             pltpu.VMEM((devices, slots, width), bf16),
             pltpu.VMEM((n_row, per_block, width), bf16),
-            pltpu.VMEM((n_col * per_block, width), f32),
             pltpu.VMEM((n_col, per_block + PACKED, width), jnp.int16),
             pltpu.VMEM((n_col, per_block + PACKED, width), jnp.int16),
             pltpu.VMEM((devices, slots, width), bf16),

time: 196 us -> 196 us (level)
  no operation moved by 1% of the time
where the time goes in v4:
time: 196 us; the launch traced here: 195 us
  Pallas kernels  185 us (94%)
  other arithmetic  5.61 us (3%)
  local copies, waits for them, and re-layouts  5.19 us (3%)
    pallas_call x1, Pallas kernels, body(): pl.pallas_call(functools.partial(kernel, n_row, n_col), out_shape=jax.Sha...  185 us

profile of v4, /device:TPU:0, one launch (start us, length us, event | category | flops | bytes accessed | tf_op | source)
XLA Modules:
  0.0 195.4 jit_solution(4059988744305904231)
XLA Ops:
  0.0 1.3 multiply_divide_fusion
  1.3 0.7 broadcast_compare_fusion
  2.0 0.8 copy.22
  2.8 0.7 subtract_subtract_fusion.rel_ref
  3.5 0.6 convert_reduce_fusion
  4.1 0.7 add_select_fusion
  4.8 0.6 select_reduce_fusion
  5.5 0.2 convert_reduce_fusion.1
  5.6 0.6 bitcast_add_fusion
  6.2 0.2 convert_reduce_fusion.2
  6.4 0.7 sub.59.back_ref
  7.1 0.7 copy.25.in_ref
  7.8 0.8 reshape.146.send_ref
  8.6 184.6 %shard_map.73 = f32[1024,256]{1,0:T(8,128)} custom-call(s32[8,3]{1,0:T(8,128)} %subtract_subtract_fusion.rel_ref, f32[1024,256]{1,0:T(8,128)} %start_ref.1, f32[8,3,128,128]{3,2,1,0:T(8,128)} %k_ref.1, s32[256,1]{1,0:T(8,128)} %reshape.146.send_ref, s32[1,256]{1,0:T(1,128)} %sub.59.back_ref, s32[128,1]{1,0:T(8,128)} %copy.25.in_ref, ...), custom_call_target="tpu_custom_call" | custom-call | tf_op jit(solution)/shard_map/pallas_call | solution.py:330
  193.2 2.3 %copy.29 = f32[1024,256]{1,0:T(8,128)} copy(f32[1024,256]{1,0:T(8,128)} %shard_map.73) | data formatting | bytes 2097152
  (6 shorter events, 0.1 us)
